TPU v7x, 256 devices: a whole 4x4x8 slice. The times are simulated.
256 devices in a mesh: row: 8 (over y, core), col: 8 (over x, z_hi), rep: 4 (over z_lo).
Axes of the slice: x: 4, y: 4, z: 8 (z_hi: 2, z_lo: 4; z = z_hi * 4 + z_lo), core: 2. Of those that a mesh axis runs over, the one named last changes fastest.
Arguments:
- features: float32 [256, 32768], P('rep', ('col', 'row')), may hold values from -6 to 6
- weight: float32 [256, 256], replicated, may hold values from -0.375 to 0.375
- cotangent: float32 [256, 32768], P('rep', ('row', 'col')), may hold values from -6 to 6
- tile_values: float32 [10240, 128, 128], P(('row', 'col')), may hold values from -0.078125 to 0.078125
- tile_row: int32 [10240], P(('row', 'col')), may hold values from 0 to 31
- tile_col: int32 [10240], P(('row', 'col')), may hold values from 0 to 31
- tile_kind: int32 [10240], P(('row', 'col')), may hold values from 0 to 159
- tile_count: int32 [64], P(('row', 'col')), may hold values from 40 to 160, as said below
Outputs:
- output: float32 [256, 32768], P('rep', ('row', 'col'))
- input_grad: float32 [256, 32768], P('rep', ('col', 'row'))
- weight_grad: float32 [256, 256], P('rep')
Inputs may be any that keep to these rules, and one draw needn't show every extreme that they name: `tile_count`: a block's slots at or after its count are not part of the adjacency; some block uses all 160 slots. `tile_row`: slots may repeat a tile position; their tiles add. `tile_kind`: an index into the 160 stored tiles of the same block.
All inputs are finite; a program needn't handle non-finite values.
Results may differ from a plain program's by a relative error of at most 0.0001.
Values sent between devices are 32-bit elements; how exact they have to be, the bound alone decides.
No kernel may reach another device: no remote copies, remote signals or barrier semaphores. Data moves between devices by JAX's collectives and lax.ppermute only.
A program may use at most 128 MiB of HBM per device.

v0:
```python
import functools

import jax
import jax.numpy as jnp
from jax import lax
from jax.experimental import pallas as pl
from jax.experimental.pallas import tpu as pltpu
from jax.sharding import PartitionSpec as P


BF16 = jnp.bfloat16
F32 = jnp.float32
NT = (((1,), (1,)), ((), ()))
NN = (((1,), (0,)), ((), ()))
GROUP = 16
CHUNK = 16
BITS = 5
ROOT_2_PI = 0.7978845608028654
CUBIC = 0.044715

dot = functools.partial(lax.dot_general, preferred_element_type=F32)


def split(x):
    high = x.astype(BF16)
    return high, (x - high.astype(F32)).astype(BF16)


def dot3(a, b, dims):
    a_high, a_low = split(a)
    b_high, b_low = split(b)
    return dot(a_high, b_high, dims) + dot(a_high, b_low, dims) + dot(a_low, b_high, dims)


def spmm_kernel(transposed, n_in, n_out, table, *refs):
    sources = refs[:n_in]
    values = refs[n_in]
    outs = refs[n_in + 1 : n_in + 1 + n_out]
    tiles, tile_sem, held, acc = refs[n_in + 1 + n_out :]
    width, length = sources[0].shape
    slots, edge, _ = values.shape
    per = length // edge
    chunks = slots // CHUNK
    count = table[slots]
    groups = (count + GROUP - 1) // GROUP

    def copy(chunk):
        at = pl.ds(chunk * CHUNK, CHUNK)
        return pltpu.make_async_copy(values.at[at], tiles.at[at], tile_sem.at[chunk])

    for c in range(chunks):
        copy(c).start()

    for b in range(n_in):
        ref = sources[b]
        for j in range(per):
            high, low = split(ref[:, j * edge : (j + 1) * edge])
            held[b * per + j, :width] = high
            held[b * per + j, width:] = low
    acc[...] = jnp.zeros_like(acc)

    def wait(chunk, carry):
        copy(chunk).wait()
        return carry

    def step(group, here):
        last = table[jnp.minimum(group * GROUP + GROUP, count) - 1]
        need = (last >> 2 * BITS) // CHUNK + 1
        lax.fori_loop(here, need, wait, 0)
        places = []
        products = []
        for u in range(GROUP):
            slot = group * GROUP + u
            packed = table[jnp.minimum(slot, count - 1)]
            kind = packed >> 2 * BITS
            by_row = (packed >> BITS) & (2**BITS - 1)
            by_col = packed & (2**BITS - 1)
            to, at = (by_col, by_row) if transposed else (by_row, by_col)
            places.append(jnp.where(slot < count, to, n_out * per))
            both = held[at]
            high, low = split(tiles[kind])
            if transposed:
                p = dot(both, high, NN)
                products.append(p[:width] + p[width:] + dot(both[:width], low, NN))
            else:
                p = dot(both, jnp.concatenate([high, low], 0), NT)
                products.append(p[:width, :edge] + p[:width, edge:] + p[width:, :edge])
        for u in range(GROUP):
            acc[places[u]] = acc[places[u]] + products[u]
        return jnp.maximum(here, need)

    here = lax.fori_loop(0, groups, step, 0)
    lax.fori_loop(here, chunks, wait, 0)
    for b in range(n_out):
        for j in range(per):
            outs[b][:, j * edge : (j + 1) * edge] = acc[b * per + j]


def spmm(table, sources, values, n_out, transposed):
    n_in = len(sources)
    width, length = sources[0].shape
    slots, edge, _ = values.shape
    per = length // edge
    vmem = pl.BlockSpec(memory_space=pltpu.VMEM)
    anywhere = pl.BlockSpec(memory_space=pl.ANY)
    return pl.pallas_call(
        functools.partial(spmm_kernel, transposed, n_in, n_out),
        in_specs=[pl.BlockSpec(memory_space=pltpu.SMEM)] + [vmem] * n_in + [anywhere],
        out_specs=[vmem] * n_out,
        out_shape=[jax.ShapeDtypeStruct((width, length), F32)] * n_out,
        scratch_shapes=[
            pltpu.VMEM((slots, edge, edge), F32),
            pltpu.SemaphoreType.DMA((slots // CHUNK,)),
            pltpu.VMEM((n_in * per, 2 * width, edge), BF16),
            pltpu.VMEM((n_out * per + 1, width, edge), F32),
        ],
        compiler_params=pltpu.CompilerParams(vmem_limit_bytes=51 << 20),
        cost_estimate=pl.CostEstimate(
            flops=6 * slots * width * edge * edge, bytes_accessed=14 << 20, transcendentals=0
        ),
        name="spmm_back" if transposed else "spmm",
    )(table, *sources, values)


def stage_kernel(source, out):
    out[...] = source[...]


def stage(x):
    vmem = pl.BlockSpec(memory_space=pltpu.VMEM)
    return pl.pallas_call(
        stage_kernel,
        in_specs=[vmem],
        out_specs=vmem,
        out_shape=jax.ShapeDtypeStruct(x.shape, x.dtype),
        compiler_params=pltpu.CompilerParams(vmem_limit_bytes=4 << 20),
        cost_estimate=pl.CostEstimate(flops=0, bytes_accessed=1 << 18, transcendentals=0),
        name="stage",
    )(x)


def mid_kernel(n_rep, scale, place, *refs):
    aggs = refs[:n_rep]
    cots = refs[n_rep : 2 * n_rep]
    weight, weight_t, out, mixed_grad, sent = refs[2 * n_rep : 2 * n_rep + 5]
    agg, cot, act = refs[2 * n_rep + 5 :]
    quarter = aggs[0].shape[0]
    me = place[0]
    for k in range(n_rep):
        at = pl.ds(pl.multiple_of((me ^ k) * quarter, quarter), quarter)
        agg[at, :] = aggs[k][...]
        cot[at, :] = cots[k][...]
    pre = dot3(weight_t[...], agg[...], NN)
    square = pre * pre
    curve = jnp.tanh(ROOT_2_PI * (pre + CUBIC * (square * pre)))
    half = 0.5 * (1.0 + curve)
    act[...] = pre * half
    slope = half + 0.5 * pre * (1.0 - curve * curve) * (
        ROOT_2_PI * (1.0 + 3.0 * CUBIC * square)
    )
    grad = cot[...] * slope
    own = pl.ds(pl.multiple_of(me * quarter, quarter), quarter)
    mine = dot3(weight[own, :], grad, NN)
    length = mine.shape[1]
    mixed_grad[...] = mine
    sent[:, :length] = mine
    sent[:, length:] = dot3(agg[own, :], grad, NT) * scale
    out[...] = act[own, :]


def mid(place, aggs, cots, weight, weight_t, scale):
    n_rep = len(aggs)
    quarter, length = aggs[0].shape
    width = weight.shape[0]
    vmem = pl.BlockSpec(memory_space=pltpu.VMEM)
    return pl.pallas_call(
        functools.partial(mid_kernel, n_rep, scale),
        in_specs=[pl.BlockSpec(memory_space=pltpu.SMEM)] + [vmem] * (2 * n_rep + 2),
        out_specs=[vmem] * 3,
        out_shape=[
            jax.ShapeDtypeStruct((quarter, length), F32),
            jax.ShapeDtypeStruct((quarter, length), F32),
            jax.ShapeDtypeStruct((quarter, length + width), F32),
        ],
        scratch_shapes=[pltpu.VMEM((width, length), F32)] * 3,
        compiler_params=pltpu.CompilerParams(vmem_limit_bytes=16 << 20),
        cost_estimate=pl.CostEstimate(
            flops=8 * width * width * length, bytes_accessed=4 << 20, transcendentals=0
        ),
        name="mid",
    )(place, *aggs, *cots, weight, weight_t)


def shift(x, axis, by):
    n = lax.axis_size(axis)
    return lax.ppermute(x, axis, [(i, (i + by) % n) for i in range(n)])


def swap(x, axis, bit):
    n = lax.axis_size(axis)
    return lax.ppermute(x, axis, [(i, i ^ bit) for i in range(n)])


def layer(features, weight, cotangent, tile_values, tile_row, tile_col, tile_kind, tile_count):
    n_row, n_col, n_rep = (lax.axis_size(a) for a in ("row", "col", "rep"))
    row, col, rep = (lax.axis_index(a) for a in ("row", "col", "rep"))
    stretch = features.shape[1]
    per = stretch // tile_values.shape[1]
    slots = tile_kind.shape[0]

    def relative(tile, at, n):
        stretch_of = tile // per
        far = (stretch_of // 2 - at // 2) % (n // 2)
        return (far * 2 + ((stretch_of ^ at) & 1)) * per + tile % per

    by_row = relative(tile_row, col, n_col)
    by_col = relative(tile_col, row, n_row)
    ids = jnp.arange(slots, dtype=jnp.int32)
    packed = (tile_kind << 2 * BITS) + (by_row << BITS) + by_col
    key = jnp.where(ids < tile_count[0], tile_kind, slots) * slots + ids
    rank = jnp.sum((key[None, :] < key[:, None]).astype(jnp.int32), axis=1)
    ordered = jnp.sum(jnp.where(rank[None, :] == ids[:, None], packed[None, :], 0), axis=1)
    table = jnp.concatenate([ordered, tile_count])
    blocks = []
    for k in range(n_row // 2):
        mine = shift(features, "row", -2 * k) if k else features
        blocks += [mine, swap(mine, "row", 1)]
    blocks[0] = stage(features)
    cots = [cotangent]
    for k in range(1, n_rep):
        cots.append(swap(cotangent, "rep", k))
    parts = spmm(table, blocks, tile_values, n_col, False)
    sums = [None, None]
    for z in (1, 0):
        total = parts[z]
        for k in range(1, n_col // 2):
            got = shift(parts[2 * k + z], "col", 2 * k)
            total = total + got
        sums[z] = total
    far = swap(sums[1], "col", 1)
    agg = sums[0] + far
    aggs = [agg] + [swap(agg, "rep", k) for k in range(1, n_rep)]
    place = rep.astype(jnp.int32)[None]
    node_total = stretch * n_row * n_col
    output, mixed_grad, sent = mid(
        place, aggs, cots, weight, weight.T, float(node_total) ** (-0.5)
    )
    far = swap(mixed_grad, "col", 1)
    blocks = [mixed_grad, far]
    weight_grad = sent[:, stretch:]
    for k in range(1, n_col // 2):
        got = shift(sent, "col", -2 * k)
        weight_grad = weight_grad + got[:, stretch:]
        blocks += [got, shift(far, "col", -2 * k)]

    def add_swapped(x, axis, bit):
        return x + swap(x, axis, bit)

    weight_grad = add_swapped(weight_grad, "col", 1)
    parts = spmm(table, blocks, tile_values, n_row, True)
    totals = []
    for k in range(n_row // 2):
        got = swap(parts[2 * k + 1], "row", 1)
        totals.append(parts[2 * k] + got)
    input_grad = totals[0]
    for k in (2, 1, 3):
        got = shift(totals[k], "row", 2 * k)
        input_grad = input_grad + got
    weight_grad = add_swapped(weight_grad, "row", 1)
    weight_grad = add_swapped(weight_grad, "row", 2)
    weight_grad = add_swapped(weight_grad, "row", 4)
    return (output, input_grad, weight_grad)


def solution(mesh):
    return jax.shard_map(
        layer,
        mesh=mesh,
        in_specs=(
            P("rep", ("col", "row")),
            P(),
            P("rep", ("row", "col")),
            P(("row", "col"), None, None),
            P(("row", "col")),
            P(("row", "col")),
            P(("row", "col")),
            P(("row", "col")),
        ),
        out_specs=(P("rep", ("row", "col")), P("rep", ("col", "row")), P("rep", None)),
        check_vma=False,
    )
```

profile of v0, /device:TPU:40, one launch (start us, length us, event | category | flops | bytes accessed | tf_op | source)
XLA Modules:
  0.0 117.5 jit_solution(1639860226693294973)
XLA Ops:
  1.2 2.6 %collective-permute-start.3 = (f32[64,512]{1,0:T(8,128)}, f32[64,512]{1,0:T(8,128)S(1)}, u32[]{:S(2)}, u32[]{:S(2)}) collective-permute-start(f32[64,512]{1,0:T(8,128)} %source.1), channel_id=1, source_target_pairs={{0,128},{32,160},{64,192},{96,224},{128,0},{160,32},{192,64},{224,... | collective-permute-start | bytes 393224 | tf_op jit(solution)/shard_map/ppermute | solution.py:196
  3.8 1.9 %collective-permute-start.5 = (f32[64,512]{1,0:T(8,128)}, f32[64,512]{1,0:T(8,128)S(1)}, u32[]{:S(2)}, u32[]{:S(2)}) collective-permute-start(f32[64,512]{1,0:T(8,128)} %source.1), channel_id=1, source_target_pairs={{0,64},{32,96},{64,128},{96,160},{128,192},{160,224},{192,0},{224,... | collective-permute-start | bytes 393224 | tf_op jit(solution)/shard_map/ppermute | solution.py:196
  7.9 2.1 %collective-permute-done.3.refs_4_ = f32[64,512]{1,0:T(8,128)S(1)} collective-permute-done((f32[64,512]{1,0:T(8,128)}, f32[64,512]{1,0:T(8,128)S(1)}, u32[]{:S(2)}, u32[]{:S(2)}) %collective-permute-start.3) | collective-permute-done | bytes 131104 | tf_op jit(solution)/shard_map/ppermute | solution.py:196
  12.1 5.6 %spmm.1 = (f32[64,512]{1,0:T(8,128)S(1)}, f32[64,512]{1,0:T(8,128)S(1)}, f32[64,512]{1,0:T(8,128)S(1)}, f32[64,512]{1,0:T(8,128)S(1)}, f32[64,512]{1,0:T(8,128)S...) custom-call(s32[161]{0:T(256)S(1)} %pad_add_fusion.table, f32[64,512]{1,0:T(8,128)S(1)} %stage.1.refs_0_, ...), custom_call_target="tpu_custom_call" | custom-call | flops 1006632960 | bytes 14680064 | tf_op jit(solution)/shard_map/spmm/pallas_call | solution.py:106
  17.8 2.9 %collective-permute-start.10 = (f32[64,512]{1,0:T(8,128)S(1)}, f32[64,512]{1,0:T(8,128)S(1)}, u32[]{:S(2)}, u32[]{:S(2)}) collective-permute-start(f32[64,512]{1,0:T(8,128)S(1)} %get-tuple-element.27), channel_id=1, source_target_pairs={{0,8},{4,12},{8,16},{12,20},{16,24},{20,28},{24,0},{28,4},{1,9},{5... | collective-permute-start | bytes 393224 | tf_op jit(solution)/shard_map/ppermute | solution.py:196
  20.7 2.2 %collective-permute-start.11 = (f32[64,512]{1,0:T(8,128)S(1)}, f32[64,512]{1,0:T(8,128)S(1)}, u32[]{:S(2)}, u32[]{:S(2)}) collective-permute-start(f32[64,512]{1,0:T(8,128)S(1)} %get-tuple-element.28), channel_id=1, source_target_pairs={{0,16},{4,20},{8,24},{12,28},{16,0},{20,4},{24,8},{28,12},{1,17},{... | collective-permute-start | bytes 393224 | tf_op jit(solution)/shard_map/ppermute | solution.py:196
  23.0 1.4 %collective-permute-start.12 = (f32[64,512]{1,0:T(8,128)S(1)}, f32[64,512]{1,0:T(8,128)S(1)}, u32[]{:S(2)}, u32[]{:S(2)}) collective-permute-start(f32[64,512]{1,0:T(8,128)S(1)} %get-tuple-element.29), channel_id=1, source_target_pairs={{0,24},{4,28},{8,0},{12,4},{16,8},{20,12},{24,16},{28,20},{1,25},{... | collective-permute-start | bytes 393224 | tf_op jit(solution)/shard_map/ppermute | solution.py:196
  25.0 1.3 %collective-permute-start.8 = (f32[64,512]{1,0:T(8,128)S(1)}, f32[64,512]{1,0:T(8,128)S(1)}, u32[]{:S(2)}, u32[]{:S(2)}) collective-permute-start(f32[64,512]{1,0:T(8,128)S(1)} %get-tuple-element.24), channel_id=1, source_target_pairs={{0,16},{4,20},{8,24},{12,28},{16,0},{20,4},{24,8},{28,12},{1,17},{... | collective-permute-start | bytes 393224 | tf_op jit(solution)/shard_map/ppermute | solution.py:196
  26.3 1.6 %collective-permute-start.9 = (f32[64,512]{1,0:T(8,128)S(1)}, f32[64,512]{1,0:T(8,128)S(1)}, u32[]{:S(2)}, u32[]{:S(2)}) collective-permute-start(f32[64,512]{1,0:T(8,128)S(1)} %get-tuple-element.25), channel_id=1, source_target_pairs={{0,24},{4,28},{8,0},{12,4},{16,8},{20,12},{24,16},{28,20},{1,25},{... | collective-permute-start | bytes 393224 | tf_op jit(solution)/shard_map/ppermute | solution.py:196
  27.9 2.2 %collective-permute-done.11 = f32[64,512]{1,0:T(8,128)S(1)} collective-permute-done((f32[64,512]{1,0:T(8,128)S(1)}, f32[64,512]{1,0:T(8,128)S(1)}, u32[]{:S(2)}, u32[]{:S(2)}) %collective-permute-start.11) | collective-permute-done | bytes 131104 | tf_op jit(solution)/shard_map/ppermute | solution.py:196
  30.2 6.8 %collective-permute-start.13 = (f32[64,512]{1,0:T(8,128)S(1)}, f32[64,512]{1,0:T(8,128)S(1)}, u32[]{:S(2)}, u32[]{:S(2)}) collective-permute-start(f32[64,512]{1,0:T(8,128)S(1)} %add_add_fusion.1), channel_id=1, source_target_pairs={{0,4},{4,0},{8,12},{12,8},{16,20},{20,16},{24,28},{28,24},{1,5},{5... | collective-permute-start | bytes 393224 | tf_op jit(solution)/shard_map/ppermute | solution.py:201
  38.0 1.4 %collective-permute-start.18 = (f32[64,512]{1,0:T(8,128)S(1)}, f32[64,512]{1,0:T(8,128)S(1)}, u32[]{:S(2)}, u32[]{:S(2)}) collective-permute-start(f32[64,512]{1,0:T(8,128)S(1)} %copy-done.1), channel_id=1, source_target_pairs={{0,2},{1,3},{2,0},{3,1},{4,6},{5,7},{6,4},{7,5},{8,10},{9,11},{10,... | collective-permute-start | bytes 393224 | tf_op jit(solution)/shard_map/ppermute | solution.py:201
  39.4 1.0 collective-permute-start.19
  40.4 2.8 %collective-permute-done.13 = f32[64,512]{1,0:T(8,128)S(1)} collective-permute-done((f32[64,512]{1,0:T(8,128)S(1)}, f32[64,512]{1,0:T(8,128)S(1)}, u32[]{:S(2)}, u32[]{:S(2)}) %collective-permute-start.13) | collective-permute-done | bytes 131104 | tf_op jit(solution)/shard_map/ppermute | solution.py:201
  43.5 2.3 %collective-permute-start.15 = (f32[64,512]{1,0:T(8,128)S(1)}, f32[64,512]{1,0:T(8,128)S(1)}, u32[]{:S(2)}, u32[]{:S(2)}) collective-permute-start(f32[64,512]{1,0:T(8,128)S(1)} %add_add_fusion.2.refs_0_), channel_id=1, source_target_pairs={{0,2},{1,3},{2,0},{3,1},{4,6},{5,7},{6,4},{7,5},{8,10},{9,11},{10,... | collective-permute-start | bytes 393224 | tf_op jit(solution)/shard_map/ppermute | solution.py:201
  45.8 3.0 %collective-permute-done.17.refs_5_ = f32[64,512]{1,0:T(8,128)S(1)} collective-permute-done((f32[64,512]{1,0:T(8,128)S(1)}, f32[64,512]{1,0:T(8,128)S(1)}, u32[]{:S(2)}, u32[]{:S(2)}) %collective-permute-start.17) | collective-permute-done | bytes 131104 | tf_op jit(solution)/shard_map/ppermute | solution.py:201
  49.6 9.6 %collective-permute-done.19.refs_7_ = f32[64,512]{1,0:T(8,128)S(1)} collective-permute-done((f32[64,512]{1,0:T(8,128)S(1)}, f32[64,512]{1,0:T(8,128)S(1)}, u32[]{:S(2)}, u32[]{:S(2)}) %collective-permute-start.19) | collective-permute-done | bytes 131104 | tf_op jit(solution)/shard_map/ppermute | solution.py:201
  59.2 1.6 %collective-permute-done.15.refs_2_ = f32[64,512]{1,0:T(8,128)S(1)} collective-permute-done((f32[64,512]{1,0:T(8,128)S(1)}, f32[64,512]{1,0:T(8,128)S(1)}, u32[]{:S(2)}, u32[]{:S(2)}) %collective-permute-start.15) | collective-permute-done | bytes 131104 | tf_op jit(solution)/shard_map/ppermute | solution.py:201
  60.8 2.7 %collective-permute-done.16.refs_3_ = f32[64,512]{1,0:T(8,128)S(1)} collective-permute-done((f32[64,512]{1,0:T(8,128)S(1)}, f32[64,512]{1,0:T(8,128)S(1)}, u32[]{:S(2)}, u32[]{:S(2)}) %collective-permute-start.16) | collective-permute-done | bytes 131104 | tf_op jit(solution)/shard_map/ppermute | solution.py:201
  63.5 1.9 %mid.1 = (f32[64,512]{1,0:T(8,128)}, f32[64,512]{1,0:T(8,128)S(1)}, f32[64,768]{1,0:T(8,128)S(1)}) custom-call(s32[1]{0:T(128)} %bitcast.place, f32[64,512]{1,0:T(8,128)S(1)} %add_add_fusion.2.refs_0_, f32[64,512]{1,0:T(8,128)S(1)} %collective-permute-done.14.refs_1_, f32[64,512]{1,0:T(8,128)S(1)} %collective-permute-done.15.refs_2_, ...), custom_call_target="tpu_custom_call" | custom-call | flops 268435456 | bytes 4194304 | tf_op jit(solution)/shard_map/mid/pallas_call | solution.py:176
  65.4 6.5 %collective-permute-start.21 = (f32[64,768]{1,0:T(8,128)S(1)}, f32[64,768]{1,0:T(8,128)S(1)}, u32[]{:S(2)}, u32[]{:S(2)}) collective-permute-start(f32[64,768]{1,0:T(8,128)S(1)} %get-tuple-element.32), channel_id=1, source_target_pairs={{0,24},{4,28},{8,0},{12,4},{16,8},{20,12},{24,16},{28,20},{1,25},{... | collective-permute-start | bytes 589832 | tf_op jit(solution)/shard_map/ppermute | solution.py:196
  72.7 1.4 %collective-permute-start.20 = (f32[64,512]{1,0:T(8,128)S(1)}, f32[64,512]{1,0:T(8,128)S(1)}, u32[]{:S(2)}, u32[]{:S(2)}) collective-permute-start(f32[64,512]{1,0:T(8,128)S(1)} %get-tuple-element.31.refs_0_), channel_id=1, source_target_pairs={{0,4},{4,0},{8,12},{12,8},{16,20},{20,16},{24,28},{28,24},{1,5},{5... | collective-permute-start | bytes 393224 | tf_op jit(solution)/shard_map/ppermute | solution.py:201
  74.1 8.7 %collective-permute-done.20.refs_1_ = f32[64,512]{1,0:T(8,128)S(1)} collective-permute-done((f32[64,512]{1,0:T(8,128)S(1)}, f32[64,512]{1,0:T(8,128)S(1)}, u32[]{:S(2)}, u32[]{:S(2)}) %collective-permute-start.20) | collective-permute-done | bytes 131104 | tf_op jit(solution)/shard_map/ppermute | solution.py:201
  82.8 2.4 %collective-permute-start.22 = (f32[64,512]{1,0:T(8,128)S(1)}, f32[64,512]{1,0:T(8,128)S(1)}, u32[]{:S(2)}, u32[]{:S(2)}) collective-permute-start(f32[64,512]{1,0:T(8,128)S(1)} %collective-permute-done.20.refs_1_), channel_id=1, source_target_pairs={{0,24},{4,28},{8,0},{12,4},{16,8},{20,12},{24,16},{28,20},{1,25},{... | collective-permute-start | bytes 393224 | tf_op jit(solution)/shard_map/ppermute | solution.py:196
  85.1 2.3 %collective-permute-start.24 = (f32[64,512]{1,0:T(8,128)S(1)}, f32[64,512]{1,0:T(8,128)S(1)}, u32[]{:S(2)}, u32[]{:S(2)}) collective-permute-start(f32[64,512]{1,0:T(8,128)S(1)} %collective-permute-done.20.refs_1_), channel_id=1, source_target_pairs={{0,16},{4,20},{8,24},{12,28},{16,0},{20,4},{24,8},{28,12},{1,17},{... | collective-permute-start | bytes 393224 | tf_op jit(solution)/shard_map/ppermute | solution.py:196
  88.3 3.3 %collective-permute-done.24.refs_5_ = f32[64,512]{1,0:T(8,128)S(1)} collective-permute-done((f32[64,512]{1,0:T(8,128)S(1)}, f32[64,512]{1,0:T(8,128)S(1)}, u32[]{:S(2)}, u32[]{:S(2)}) %collective-permute-start.24) | collective-permute-done | bytes 131104 | tf_op jit(solution)/shard_map/ppermute | solution.py:196
  91.6 2.0 %collective-permute-done.26.refs_7_ = f32[64,512]{1,0:T(8,128)S(1)} collective-permute-done((f32[64,512]{1,0:T(8,128)S(1)}, f32[64,512]{1,0:T(8,128)S(1)}, u32[]{:S(2)}, u32[]{:S(2)}) %collective-permute-start.26) | collective-permute-done | bytes 131104 | tf_op jit(solution)/shard_map/ppermute | solution.py:196
  93.6 5.6 %spmm_back.1 = (f32[64,512]{1,0:T(8,128)S(1)}, f32[64,512]{1,0:T(8,128)S(1)}, f32[64,512]{1,0:T(8,128)S(1)}, f32[64,512]{1,0:T(8,128)S(1)}, f32[64,512]{1,0:T(8,...) custom-call(s32[161]{0:T(256)S(1)} %pad_add_fusion.table, ...), custom_call_target="tpu_custom_call" | custom-call | flops 1006632960 | bytes 14680064 | tf_op jit(solution)/shard_map/spmm_back/pallas_call | solution.py:106
  101.4 3.4 %collective-permute-start.36 = (f32[64,256]{1,0:T(8,128)S(1)}, f32[64,256]{1,0:T(8,128)S(1)}, u32[]{:S(2)}, u32[]{:S(2)}) collective-permute-start(f32[64,256]{1,0:T(8,128)S(1)} %add.137), channel_id=1, source_target_pairs={{0,64},{32,96},{64,0},{96,32},{128,192},{160,224},{192,128},{224,1... | collective-permute-start | bytes 196616 | tf_op jit(solution)/shard_map/ppermute | solution.py:201
  104.9 1.5 %collective-permute-start.31 = (f32[64,512]{1,0:T(8,128)S(1)}, f32[64,512]{1,0:T(8,128)S(1)}, u32[]{:S(2)}, u32[]{:S(2)}) collective-permute-start(f32[64,512]{1,0:T(8,128)S(1)} %add.129), channel_id=1, source_target_pairs={{0,64},{32,96},{64,128},{96,160},{128,192},{160,224},{192,0},{224,... | collective-permute-start | bytes 393224 | tf_op jit(solution)/shard_map/ppermute | solution.py:196
  107.7 3.0 %collective-permute-start.37 = (f32[64,256]{1,0:T(8,128)S(1)}, f32[64,256]{1,0:T(8,128)S(1)}, u32[]{:S(2)}, u32[]{:S(2)}) collective-permute-start(f32[64,256]{1,0:T(8,128)S(1)} %add.138), channel_id=1, source_target_pairs={{0,128},{32,160},{64,192},{96,224},{128,0},{160,32},{192,64},{224,... | collective-permute-start | bytes 196616 | tf_op jit(solution)/shard_map/ppermute | solution.py:201
  110.8 5.3 %collective-permute-done.37 = f32[64,256]{1,0:T(8,128)S(1)} collective-permute-done((f32[64,256]{1,0:T(8,128)S(1)}, f32[64,256]{1,0:T(8,128)S(1)}, u32[]{:S(2)}, u32[]{:S(2)}) %collective-permute-start.37) | collective-permute-done | bytes 65568 | tf_op jit(solution)/shard_map/ppermute | solution.py:201
  (70 shorter events, 13.5 us)
Async XLA Ops:
  0.7 6.6 %collective-permute-start.1 = (f32[64,512]{1,0:T(8,128)}, f32[64,512]{1,0:T(8,128)S(1)}, u32[]{:S(2)}, u32[]{:S(2)}) collective-permute-start(f32[64,512]{1,0:T(8,128)} %source.1), channel_id=1, source_target_pairs={{0,192},{32,224},{64,0},{96,32},{128,64},{160,96},{192,128},{224,1... | collective-permute-start | bytes 393224 | tf_op jit(solution)/shard_map/ppermute | solution.py:196
  1.2 8.8 %collective-permute-start.3 = (f32[64,512]{1,0:T(8,128)}, f32[64,512]{1,0:T(8,128)S(1)}, u32[]{:S(2)}, u32[]{:S(2)}) collective-permute-start(f32[64,512]{1,0:T(8,128)} %source.1), channel_id=1, source_target_pairs={{0,128},{32,160},{64,192},{96,224},{128,0},{160,32},{192,64},{224,... | collective-permute-start | bytes 393224 | tf_op jit(solution)/shard_map/ppermute | solution.py:196
  3.8 7.0 %collective-permute-start.5 = (f32[64,512]{1,0:T(8,128)}, f32[64,512]{1,0:T(8,128)S(1)}, u32[]{:S(2)}, u32[]{:S(2)}) collective-permute-start(f32[64,512]{1,0:T(8,128)} %source.1), channel_id=1, source_target_pairs={{0,64},{32,96},{64,128},{96,160},{128,192},{160,224},{192,0},{224,... | collective-permute-start | bytes 393224 | tf_op jit(solution)/shard_map/ppermute | solution.py:196
  5.7 6.2 %collective-permute-start = (f32[64,512]{1,0:T(8,128)}, f32[64,512]{1,0:T(8,128)S(1)}, u32[]{:S(2)}, u32[]{:S(2)}) collective-permute-start(f32[64,512]{1,0:T(8,128)} %source.1), channel_id=1, source_target_pairs={{0,32},{32,0},{64,96},{96,64},{128,160},{160,128},{192,224},{224,1... | collective-permute-start | bytes 393224 | tf_op jit(solution)/shard_map/ppermute | solution.py:201
  17.8 8.5 %collective-permute-start.10 = (f32[64,512]{1,0:T(8,128)S(1)}, f32[64,512]{1,0:T(8,128)S(1)}, u32[]{:S(2)}, u32[]{:S(2)}) collective-permute-start(f32[64,512]{1,0:T(8,128)S(1)} %get-tuple-element.27), channel_id=1, source_target_pairs={{0,8},{4,12},{8,16},{12,20},{16,24},{20,28},{24,0},{28,4},{1,9},{5... | collective-permute-start | bytes 393224 | tf_op jit(solution)/shard_map/ppermute | solution.py:196
  20.7 9.4 %collective-permute-start.11 = (f32[64,512]{1,0:T(8,128)S(1)}, f32[64,512]{1,0:T(8,128)S(1)}, u32[]{:S(2)}, u32[]{:S(2)}) collective-permute-start(f32[64,512]{1,0:T(8,128)S(1)} %get-tuple-element.28), channel_id=1, source_target_pairs={{0,16},{4,20},{8,24},{12,28},{16,0},{20,4},{24,8},{28,12},{1,17},{... | collective-permute-start | bytes 393224 | tf_op jit(solution)/shard_map/ppermute | solution.py:196
  23.0 7.2 %collective-permute-start.12 = (f32[64,512]{1,0:T(8,128)S(1)}, f32[64,512]{1,0:T(8,128)S(1)}, u32[]{:S(2)}, u32[]{:S(2)}) collective-permute-start(f32[64,512]{1,0:T(8,128)S(1)} %get-tuple-element.29), channel_id=1, source_target_pairs={{0,24},{4,28},{8,0},{12,4},{16,8},{20,12},{24,16},{28,20},{1,25},{... | collective-permute-start | bytes 393224 | tf_op jit(solution)/shard_map/ppermute | solution.py:196
  24.4 13.5 %collective-permute-start.7 = (f32[64,512]{1,0:T(8,128)S(1)}, f32[64,512]{1,0:T(8,128)S(1)}, u32[]{:S(2)}, u32[]{:S(2)}) collective-permute-start(f32[64,512]{1,0:T(8,128)S(1)} %get-tuple-element.23), channel_id=1, source_target_pairs={{0,8},{4,12},{8,16},{12,20},{16,24},{20,28},{24,0},{28,4},{1,9},{5... | collective-permute-start | bytes 393224 | tf_op jit(solution)/shard_map/ppermute | solution.py:196
  25.0 14.4 %collective-permute-start.8 = (f32[64,512]{1,0:T(8,128)S(1)}, f32[64,512]{1,0:T(8,128)S(1)}, u32[]{:S(2)}, u32[]{:S(2)}) collective-permute-start(f32[64,512]{1,0:T(8,128)S(1)} %get-tuple-element.24), channel_id=1, source_target_pairs={{0,16},{4,20},{8,24},{12,28},{16,0},{20,4},{24,8},{28,12},{1,17},{... | collective-permute-start | bytes 393224 | tf_op jit(solution)/shard_map/ppermute | solution.py:196
  26.3 14.1 %collective-permute-start.9 = (f32[64,512]{1,0:T(8,128)S(1)}, f32[64,512]{1,0:T(8,128)S(1)}, u32[]{:S(2)}, u32[]{:S(2)}) collective-permute-start(f32[64,512]{1,0:T(8,128)S(1)} %get-tuple-element.25), channel_id=1, source_target_pairs={{0,24},{4,28},{8,0},{12,4},{16,8},{20,12},{24,16},{28,20},{1,25},{... | collective-permute-start | bytes 393224 | tf_op jit(solution)/shard_map/ppermute | solution.py:196
  30.2 13.0 %collective-permute-start.13 = (f32[64,512]{1,0:T(8,128)S(1)}, f32[64,512]{1,0:T(8,128)S(1)}, u32[]{:S(2)}, u32[]{:S(2)}) collective-permute-start(f32[64,512]{1,0:T(8,128)S(1)} %add_add_fusion.1), channel_id=1, source_target_pairs={{0,4},{4,0},{8,12},{12,8},{16,20},{20,16},{24,28},{28,24},{1,5},{5... | collective-permute-start | bytes 393224 | tf_op jit(solution)/shard_map/ppermute | solution.py:201
  36.9 11.9 %collective-permute-start.17 = (f32[64,512]{1,0:T(8,128)S(1)}, f32[64,512]{1,0:T(8,128)S(1)}, u32[]{:S(2)}, u32[]{:S(2)}) collective-permute-start(f32[64,512]{1,0:T(8,128)S(1)} %copy-done.1), channel_id=1, source_target_pairs={{0,1},{1,0},{2,3},{3,2},{4,5},{5,4},{6,7},{7,6},{8,9},{9,8},{10,11... | collective-permute-start | bytes 393224 | tf_op jit(solution)/shard_map/ppermute | solution.py:201
  38.0 11.6 %collective-permute-start.18 = (f32[64,512]{1,0:T(8,128)S(1)}, f32[64,512]{1,0:T(8,128)S(1)}, u32[]{:S(2)}, u32[]{:S(2)}) collective-permute-start(f32[64,512]{1,0:T(8,128)S(1)} %copy-done.1), channel_id=1, source_target_pairs={{0,2},{1,3},{2,0},{3,1},{4,6},{5,7},{6,4},{7,5},{8,10},{9,11},{10,... | collective-permute-start | bytes 393224 | tf_op jit(solution)/shard_map/ppermute | solution.py:201
  39.4 19.8 %collective-permute-start.19 = (f32[64,512]{1,0:T(8,128)S(1)}, f32[64,512]{1,0:T(8,128)S(1)}, u32[]{:S(2)}, u32[]{:S(2)}) collective-permute-start(f32[64,512]{1,0:T(8,128)S(1)} %copy-done.1), channel_id=1, source_target_pairs={{0,3},{1,2},{2,1},{3,0},{4,7},{5,6},{6,5},{7,4},{8,11},{9,10},{10,... | collective-permute-start | bytes 393224 | tf_op jit(solution)/shard_map/ppermute | solution.py:201
  43.3 16.0 %collective-permute-start.14 = (f32[64,512]{1,0:T(8,128)S(1)}, f32[64,512]{1,0:T(8,128)S(1)}, u32[]{:S(2)}, u32[]{:S(2)}) collective-permute-start(f32[64,512]{1,0:T(8,128)S(1)} %add_add_fusion.2.refs_0_), channel_id=1, source_target_pairs={{0,1},{1,0},{2,3},{3,2},{4,5},{5,4},{6,7},{7,6},{8,9},{9,8},{10,11... | collective-permute-start | bytes 393224 | tf_op jit(solution)/shard_map/ppermute | solution.py:201
  43.5 17.2 %collective-permute-start.15 = (f32[64,512]{1,0:T(8,128)S(1)}, f32[64,512]{1,0:T(8,128)S(1)}, u32[]{:S(2)}, u32[]{:S(2)}) collective-permute-start(f32[64,512]{1,0:T(8,128)S(1)} %add_add_fusion.2.refs_0_), channel_id=1, source_target_pairs={{0,2},{1,3},{2,0},{3,1},{4,6},{5,7},{6,4},{7,5},{8,10},{9,11},{10,... | collective-permute-start | bytes 393224 | tf_op jit(solution)/shard_map/ppermute | solution.py:201
  48.8 14.7 %collective-permute-start.16 = (f32[64,512]{1,0:T(8,128)S(1)}, f32[64,512]{1,0:T(8,128)S(1)}, u32[]{:S(2)}, u32[]{:S(2)}) collective-permute-start(f32[64,512]{1,0:T(8,128)S(1)} %add_add_fusion.2.refs_0_), channel_id=1, source_target_pairs={{0,3},{1,2},{2,1},{3,0},{4,7},{5,6},{6,5},{7,4},{8,11},{9,10},{10,... | collective-permute-start | bytes 393224 | tf_op jit(solution)/shard_map/ppermute | solution.py:201
  65.4 22.1 %collective-permute-start.21 = (f32[64,768]{1,0:T(8,128)S(1)}, f32[64,768]{1,0:T(8,128)S(1)}, u32[]{:S(2)}, u32[]{:S(2)}) collective-permute-start(f32[64,768]{1,0:T(8,128)S(1)} %get-tuple-element.32), channel_id=1, source_target_pairs={{0,24},{4,28},{8,0},{12,4},{16,8},{20,12},{24,16},{28,20},{1,25},{... | collective-permute-start | bytes 589832 | tf_op jit(solution)/shard_map/ppermute | solution.py:196
  71.8 15.6 %collective-permute-start.23 = (f32[64,768]{1,0:T(8,128)S(1)}, f32[64,768]{1,0:T(8,128)S(1)}, u32[]{:S(2)}, u32[]{:S(2)}) collective-permute-start(f32[64,768]{1,0:T(8,128)S(1)} %get-tuple-element.32), channel_id=1, source_target_pairs={{0,16},{4,20},{8,24},{12,28},{16,0},{20,4},{24,8},{28,12},{1,17},{... | collective-permute-start | bytes 589832 | tf_op jit(solution)/shard_map/ppermute | solution.py:196
  71.8 15.6 %collective-permute-start.25 = (f32[64,768]{1,0:T(8,128)S(1)}, f32[64,768]{1,0:T(8,128)S(1)}, u32[]{:S(2)}, u32[]{:S(2)}) collective-permute-start(f32[64,768]{1,0:T(8,128)S(1)} %get-tuple-element.32), channel_id=1, source_target_pairs={{0,8},{4,12},{8,16},{12,20},{16,24},{20,28},{24,0},{28,4},{1,9},{5... | collective-permute-start | bytes 589832 | tf_op jit(solution)/shard_map/ppermute | solution.py:196
  72.7 10.1 %collective-permute-start.20 = (f32[64,512]{1,0:T(8,128)S(1)}, f32[64,512]{1,0:T(8,128)S(1)}, u32[]{:S(2)}, u32[]{:S(2)}) collective-permute-start(f32[64,512]{1,0:T(8,128)S(1)} %get-tuple-element.31.refs_0_), channel_id=1, source_target_pairs={{0,4},{4,0},{8,12},{12,8},{16,20},{20,16},{24,28},{28,24},{1,5},{5... | collective-permute-start | bytes 393224 | tf_op jit(solution)/shard_map/ppermute | solution.py:201
  82.8 5.6 %collective-permute-start.22 = (f32[64,512]{1,0:T(8,128)S(1)}, f32[64,512]{1,0:T(8,128)S(1)}, u32[]{:S(2)}, u32[]{:S(2)}) collective-permute-start(f32[64,512]{1,0:T(8,128)S(1)} %collective-permute-done.20.refs_1_), channel_id=1, source_target_pairs={{0,24},{4,28},{8,0},{12,4},{16,8},{20,12},{24,16},{28,20},{1,25},{... | collective-permute-start | bytes 393224 | tf_op jit(solution)/shard_map/ppermute | solution.py:196
  85.1 6.5 %collective-permute-start.24 = (f32[64,512]{1,0:T(8,128)S(1)}, f32[64,512]{1,0:T(8,128)S(1)}, u32[]{:S(2)}, u32[]{:S(2)}) collective-permute-start(f32[64,512]{1,0:T(8,128)S(1)} %collective-permute-done.20.refs_1_), channel_id=1, source_target_pairs={{0,16},{4,20},{8,24},{12,28},{16,0},{20,4},{24,8},{28,12},{1,17},{... | collective-permute-start | bytes 393224 | tf_op jit(solution)/shard_map/ppermute | solution.py:196
  87.5 6.2 %collective-permute-start.26 = (f32[64,512]{1,0:T(8,128)S(1)}, f32[64,512]{1,0:T(8,128)S(1)}, u32[]{:S(2)}, u32[]{:S(2)}) collective-permute-start(f32[64,512]{1,0:T(8,128)S(1)} %collective-permute-done.20.refs_1_), channel_id=1, source_target_pairs={{0,8},{4,12},{8,16},{12,20},{16,24},{20,28},{24,0},{28,4},{1,9},{5... | collective-permute-start | bytes 393224 | tf_op jit(solution)/shard_map/ppermute | solution.py:196
  87.5 12.5 %collective-permute-start.34 = (f32[64,256]{1,0:T(8,128)S(1)}, f32[64,256]{1,0:T(8,128)S(1)}, u32[]{:S(2)}, u32[]{:S(2)}) collective-permute-start(f32[64,256]{1,0:T(8,128)S(1)} %slice_add_fusion), channel_id=1, source_target_pairs={{0,4},{4,0},{8,12},{12,8},{16,20},{20,16},{24,28},{28,24},{1,5},{5... | collective-permute-start | bytes 196616 | tf_op jit(solution)/shard_map/ppermute | solution.py:201
  99.9 6.6 %collective-permute-start.32 = (f32[64,512]{1,0:T(8,128)S(1)}, f32[64,512]{1,0:T(8,128)S(1)}, u32[]{:S(2)}, u32[]{:S(2)}) collective-permute-start(f32[64,512]{1,0:T(8,128)S(1)} %get-tuple-element.40), channel_id=1, source_target_pairs={{0,32},{32,0},{64,96},{96,64},{128,160},{160,128},{192,224},{224,1... | collective-permute-start | bytes 393224 | tf_op jit(solution)/shard_map/ppermute | solution.py:201
  100.5 16.2 %collective-permute-start.27 = (f32[64,512]{1,0:T(8,128)S(1)}, f32[64,512]{1,0:T(8,128)S(1)}, u32[]{:S(2)}, u32[]{:S(2)}) collective-permute-start(f32[64,512]{1,0:T(8,128)S(1)} %get-tuple-element.34), channel_id=1, source_target_pairs={{0,32},{32,0},{64,96},{96,64},{128,160},{160,128},{192,224},{224,1... | collective-permute-start | bytes 393224 | tf_op jit(solution)/shard_map/ppermute | solution.py:201
  101.4 6.3 %collective-permute-start.36 = (f32[64,256]{1,0:T(8,128)S(1)}, f32[64,256]{1,0:T(8,128)S(1)}, u32[]{:S(2)}, u32[]{:S(2)}) collective-permute-start(f32[64,256]{1,0:T(8,128)S(1)} %add.137), channel_id=1, source_target_pairs={{0,64},{32,96},{64,0},{96,32},{128,192},{160,224},{192,128},{224,1... | collective-permute-start | bytes 196616 | tf_op jit(solution)/shard_map/ppermute | solution.py:201
  104.8 11.9 %collective-permute-start.29 = (f32[64,512]{1,0:T(8,128)S(1)}, f32[64,512]{1,0:T(8,128)S(1)}, u32[]{:S(2)}, u32[]{:S(2)}) collective-permute-start(f32[64,512]{1,0:T(8,128)S(1)} %add.127), channel_id=1, source_target_pairs={{0,128},{32,160},{64,192},{96,224},{128,0},{160,32},{192,64},{224,... | collective-permute-start | bytes 393224 | tf_op jit(solution)/shard_map/ppermute | solution.py:196
  104.9 11.8 %collective-permute-start.31 = (f32[64,512]{1,0:T(8,128)S(1)}, f32[64,512]{1,0:T(8,128)S(1)}, u32[]{:S(2)}, u32[]{:S(2)}) collective-permute-start(f32[64,512]{1,0:T(8,128)S(1)} %add.129), channel_id=1, source_target_pairs={{0,64},{32,96},{64,128},{96,160},{128,192},{160,224},{192,0},{224,... | collective-permute-start | bytes 393224 | tf_op jit(solution)/shard_map/ppermute | solution.py:196
  106.5 10.2 %collective-permute-start.33 = (f32[64,512]{1,0:T(8,128)S(1)}, f32[64,512]{1,0:T(8,128)S(1)}, u32[]{:S(2)}, u32[]{:S(2)}) collective-permute-start(f32[64,512]{1,0:T(8,128)S(1)} %add.131), channel_id=1, source_target_pairs={{0,192},{32,224},{64,0},{96,32},{128,64},{160,96},{192,128},{224,1... | collective-permute-start | bytes 393224 | tf_op jit(solution)/shard_map/ppermute | solution.py:196
  107.7 8.3 %collective-permute-start.37 = (f32[64,256]{1,0:T(8,128)S(1)}, f32[64,256]{1,0:T(8,128)S(1)}, u32[]{:S(2)}, u32[]{:S(2)}) collective-permute-start(f32[64,256]{1,0:T(8,128)S(1)} %add.138), channel_id=1, source_target_pairs={{0,128},{32,160},{64,192},{96,224},{128,0},{160,32},{192,64},{224,... | collective-permute-start | bytes 196616 | tf_op jit(solution)/shard_map/ppermute | solution.py:201
  (9 other events, 106.3 us)
where the time goes:
time: 118 us; the launch traced here: 117 us
  starting transfers between devices  53.4 us (45%)
  waiting for transfers between devices  45.7 us (39%)
  Pallas kernels  13.2 us (11%)
  other arithmetic  2.66 us (2%)
  between operations  1.5 us (1%)
    ppermute x20, waiting for transfers between devices, swap(): return lax.ppermute(x, axis, [(i, i ^ bit) for i in range(n)])  35.2 us
    ppermute x18, starting transfers between devices, shift(): return lax.ppermute(x, axis, [(i, (i + by) % n) for i in range(n)])  29.4 us
    ppermute x20, starting transfers between devices, swap(): return lax.ppermute(x, axis, [(i, i ^ bit) for i in range(n)])  24 us
    pallas_call x2, Pallas kernels, spmm(): pl.pallas_call(functools.partial(spmm_kernel, transposed, n_in, n_out), i...  11.3 us
    ppermute x18, waiting for transfers between devices, shift(): return lax.ppermute(x, axis, [(i, (i + by) % n) for i in range(n)])  10.5 us
  transfers between devices with their start and end apart: 38, of which 15 were waited for; matrix products, arithmetic and copies ran while one was open for 2% of the time, Pallas kernels for 5%

commit v1 on v0

--- a/solution.py
+++ b/solution.py
@@ -191,6 +191,36 @@
     )(place, *aggs, *cots, weight, weight_t)
 
 
+def join_kernel(mine, got, grad, grad_got, out):
+    length = mine.shape[1]
+    out[:, :length] = mine[...] + got[...]
+    out[:, length:] = grad[...] + grad_got[...]
+
+
+def total_kernel(n, mine, got, grad, grad_got, *refs):
+    length = mine.shape[1]
+    joined, (out, weight_out) = refs[:n], refs[n:]
+    total = mine[...] + got[...]
+    weight_total = grad[...] + grad_got[...]
+    for ref in joined:
+        total = total + ref[:, :length]
+        weight_total = weight_total + ref[:, length:]
+    out[...] = total
+    weight_out[...] = weight_total
+
+
+def small(body, shapes, *args):
+    vmem = pl.BlockSpec(memory_space=pltpu.VMEM)
+    return pl.pallas_call(
+        body,
+        in_specs=[vmem] * len(args),
+        out_specs=[vmem] * len(shapes),
+        out_shape=[jax.ShapeDtypeStruct(shape, F32) for shape in shapes],
+        compiler_params=pltpu.CompilerParams(vmem_limit_bytes=8 << 20),
+        cost_estimate=pl.CostEstimate(flops=0, bytes_accessed=1 << 19, transcendentals=0),
+    )(*args)
+
+
 def shift(x, axis, by):
     n = lax.axis_size(axis)
     return lax.ppermute(x, axis, [(i, (i + by) % n) for i in range(n)])
@@ -239,7 +269,9 @@
         sums[z] = total
     far = swap(sums[1], "col", 1)
     agg = sums[0] + far
-    aggs = [agg] + [swap(agg, "rep", k) for k in range(1, n_rep)]
+    aggs = [agg]
+    for k in range(1, n_rep):
+        aggs.append(swap(agg, "rep", k))
     place = rep.astype(jnp.int32)[None]
     node_total = stretch * n_row * n_col
     output, mixed_grad, sent = mid(
@@ -258,17 +290,22 @@
 
     weight_grad = add_swapped(weight_grad, "col", 1)
     parts = spmm(table, blocks, tile_values, n_row, True)
-    totals = []
-    for k in range(n_row // 2):
+    grad_got = swap(weight_grad, "row", 1)
+    near = None
+    joined = []
+    for k in (2, 1, 3, 0):
         got = swap(parts[2 * k + 1], "row", 1)
-        totals.append(parts[2 * k] + got)
-    input_grad = totals[0]
-    for k in (2, 1, 3):
-        got = shift(totals[k], "row", 2 * k)
-        input_grad = input_grad + got
-    weight_grad = add_swapped(weight_grad, "row", 1)
-    weight_grad = add_swapped(weight_grad, "row", 2)
-    weight_grad = add_swapped(weight_grad, "row", 4)
+        near = (parts[2 * k], got, weight_grad, grad_got)
+        if k:
+            shape = (got.shape[0], got.shape[1] + weight_grad.shape[1])
+            (total,) = small(join_kernel, [shape], *near)
+            joined.append(shift(total, "row", 2 * k))
+    input_grad, weight_grad = small(
+        functools.partial(total_kernel, len(joined)),
+        [features.shape, weight_grad.shape],
+        *near,
+        *joined,
+    )
     return (output, input_grad, weight_grad)
 
 

time: 118 us -> 119 us (level)
  the two profiles are of different devices: /device:TPU:40 before, /device:TPU:2 now
where the time goes in v1:
time: 119 us; the launch traced here: 118 us
  starting transfers between devices  51.3 us (43%)
  waiting for transfers between devices  48.4 us (41%)
  Pallas kernels  14.1 us (12%)
  between operations  1.44 us (1%)
  other arithmetic  1.25 us (1%)
    ppermute x18, waiting for transfers between devices, swap(): return lax.ppermute(x, axis, [(i, i ^ bit) for i in range(n)])  30.3 us
    ppermute x18, starting transfers between devices, shift(): return lax.ppermute(x, axis, [(i, (i + by) % n) for i in range(n)])  28.5 us
    ppermute x18, starting transfers between devices, swap(): return lax.ppermute(x, axis, [(i, i ^ bit) for i in range(n)])  22.8 us
    ppermute x18, waiting for transfers between devices, shift(): return lax.ppermute(x, axis, [(i, (i + by) % n) for i in range(n)])  18.1 us
    pallas_call x2, Pallas kernels, spmm(): pl.pallas_call(functools.partial(spmm_kernel, transposed, n_in, n_out), i...  11.4 us
  transfers between devices with their start and end apart: 36, of which 14 were waited for; matrix products, arithmetic and copies ran while one was open for 1% of the time, Pallas kernels for 5%

profile of v1, /device:TPU:2, one launch (start us, length us, event | category | flops | bytes accessed | tf_op | source)
XLA Modules:
  0.0 117.5 jit_solution(10311500903315026434)
XLA Ops:
  0.7 3.1 %collective-permute-start.1 = (f32[64,512]{1,0:T(8,128)}, f32[64,512]{1,0:T(8,128)S(1)}, u32[]{:S(2)}, u32[]{:S(2)}) collective-permute-start(f32[64,512]{1,0:T(8,128)} %source.1), channel_id=1, source_target_pairs={{0,192},{32,224},{64,0},{96,32},{128,64},{160,96},{192,128},{224,1... | collective-permute-start | bytes 393224 | tf_op jit(solution)/shard_map/ppermute | solution.py:226
  3.8 2.2 %collective-permute-start.3 = (f32[64,512]{1,0:T(8,128)}, f32[64,512]{1,0:T(8,128)S(1)}, u32[]{:S(2)}, u32[]{:S(2)}) collective-permute-start(f32[64,512]{1,0:T(8,128)} %source.1), channel_id=1, source_target_pairs={{0,128},{32,160},{64,192},{96,224},{128,0},{160,32},{192,64},{224,... | collective-permute-start | bytes 393224 | tf_op jit(solution)/shard_map/ppermute | solution.py:226
  7.7 6.2 %collective-permute-done.5.refs_6_ = f32[64,512]{1,0:T(8,128)S(1)} collective-permute-done((f32[64,512]{1,0:T(8,128)}, f32[64,512]{1,0:T(8,128)S(1)}, u32[]{:S(2)}, u32[]{:S(2)}) %collective-permute-start.5) | collective-permute-done | bytes 131104 | tf_op jit(solution)/shard_map/ppermute | solution.py:226
  15.5 5.7 %spmm.1 = (f32[64,512]{1,0:T(8,128)S(1)}, f32[64,512]{1,0:T(8,128)S(1)}, f32[64,512]{1,0:T(8,128)S(1)}, f32[64,512]{1,0:T(8,128)S(1)}, f32[64,512]{1,0:T(8,128)S...) custom-call(s32[161]{0:T(256)S(1)} %pad_add_fusion.table, f32[64,512]{1,0:T(8,128)S(1)} %stage.1.refs_0_, ...), custom_call_target="tpu_custom_call" | custom-call | flops 1006632960 | bytes 14680064 | tf_op jit(solution)/shard_map/spmm/pallas_call | solution.py:106
  21.3 2.1 %collective-permute-start.10 = (f32[64,512]{1,0:T(8,128)S(1)}, f32[64,512]{1,0:T(8,128)S(1)}, u32[]{:S(2)}, u32[]{:S(2)}) collective-permute-start(f32[64,512]{1,0:T(8,128)S(1)} %get-tuple-element.29), channel_id=1, source_target_pairs={{0,8},{4,12},{8,16},{12,20},{16,24},{20,28},{24,0},{28,4},{1,9},{5... | collective-permute-start | bytes 393224 | tf_op jit(solution)/shard_map/ppermute | solution.py:226
  23.4 1.9 %collective-permute-start.11 = (f32[64,512]{1,0:T(8,128)S(1)}, f32[64,512]{1,0:T(8,128)S(1)}, u32[]{:S(2)}, u32[]{:S(2)}) collective-permute-start(f32[64,512]{1,0:T(8,128)S(1)} %get-tuple-element.30), channel_id=1, source_target_pairs={{0,16},{4,20},{8,24},{12,28},{16,0},{20,4},{24,8},{28,12},{1,17},{... | collective-permute-start | bytes 393224 | tf_op jit(solution)/shard_map/ppermute | solution.py:226
  25.2 1.0 collective-permute-start.12
  27.2 2.9 %collective-permute-start.8 = (f32[64,512]{1,0:T(8,128)S(1)}, f32[64,512]{1,0:T(8,128)S(1)}, u32[]{:S(2)}, u32[]{:S(2)}) collective-permute-start(f32[64,512]{1,0:T(8,128)S(1)} %get-tuple-element.26), channel_id=1, source_target_pairs={{0,16},{4,20},{8,24},{12,28},{16,0},{20,4},{24,8},{28,12},{1,17},{... | collective-permute-start | bytes 393224 | tf_op jit(solution)/shard_map/ppermute | solution.py:226
  30.1 3.3 %collective-permute-start.9 = (f32[64,512]{1,0:T(8,128)S(1)}, f32[64,512]{1,0:T(8,128)S(1)}, u32[]{:S(2)}, u32[]{:S(2)}) collective-permute-start(f32[64,512]{1,0:T(8,128)S(1)} %get-tuple-element.27), channel_id=1, source_target_pairs={{0,24},{4,28},{8,0},{12,4},{16,8},{20,12},{24,16},{28,20},{1,25},{... | collective-permute-start | bytes 393224 | tf_op jit(solution)/shard_map/ppermute | solution.py:226
  34.4 6.3 %collective-permute-start.13 = (f32[64,512]{1,0:T(8,128)S(1)}, f32[64,512]{1,0:T(8,128)S(1)}, u32[]{:S(2)}, u32[]{:S(2)}) collective-permute-start(f32[64,512]{1,0:T(8,128)S(1)} %add_add_fusion), channel_id=1, source_target_pairs={{0,4},{4,0},{8,12},{12,8},{16,20},{20,16},{24,28},{28,24},{1,5},{5... | collective-permute-start | bytes 393224 | tf_op jit(solution)/shard_map/ppermute | solution.py:231
  40.7 1.5 %collective-permute-start.18 = (f32[64,512]{1,0:T(8,128)S(1)}, f32[64,512]{1,0:T(8,128)S(1)}, u32[]{:S(2)}, u32[]{:S(2)}) collective-permute-start(f32[64,512]{1,0:T(8,128)S(1)} %copy-done.1), channel_id=1, source_target_pairs={{0,2},{1,3},{2,0},{3,1},{4,6},{5,7},{6,4},{7,5},{8,10},{9,11},{10,... | collective-permute-start | bytes 393224 | tf_op jit(solution)/shard_map/ppermute | solution.py:231
  42.2 1.0 collective-permute-start.17
  43.2 1.9 %collective-permute-start.19 = (f32[64,512]{1,0:T(8,128)S(1)}, f32[64,512]{1,0:T(8,128)S(1)}, u32[]{:S(2)}, u32[]{:S(2)}) collective-permute-start(f32[64,512]{1,0:T(8,128)S(1)} %copy-done.1), channel_id=1, source_target_pairs={{0,3},{1,2},{2,1},{3,0},{4,7},{5,6},{6,5},{7,4},{8,11},{9,10},{10,... | collective-permute-start | bytes 393224 | tf_op jit(solution)/shard_map/ppermute | solution.py:231
  45.1 1.4 %collective-permute-done.13 = f32[64,512]{1,0:T(8,128)S(1)} collective-permute-done((f32[64,512]{1,0:T(8,128)S(1)}, f32[64,512]{1,0:T(8,128)S(1)}, u32[]{:S(2)}, u32[]{:S(2)}) %collective-permute-start.13) | collective-permute-done | bytes 131104 | tf_op jit(solution)/shard_map/ppermute | solution.py:231
  46.6 4.9 %collective-permute-start.16 = (f32[64,512]{1,0:T(8,128)S(1)}, f32[64,512]{1,0:T(8,128)S(1)}, u32[]{:S(2)}, u32[]{:S(2)}) collective-permute-start(f32[64,512]{1,0:T(8,128)S(1)} %add_add_fusion.1.refs_0_), channel_id=1, source_target_pairs={{0,3},{1,2},{2,1},{3,0},{4,7},{5,6},{6,5},{7,4},{8,11},{9,10},{10,... | collective-permute-start | bytes 393224 | tf_op jit(solution)/shard_map/ppermute | solution.py:231
  51.5 2.3 %collective-permute-done.18.refs_6_ = f32[64,512]{1,0:T(8,128)S(1)} collective-permute-done((f32[64,512]{1,0:T(8,128)S(1)}, f32[64,512]{1,0:T(8,128)S(1)}, u32[]{:S(2)}, u32[]{:S(2)}) %collective-permute-start.18) | collective-permute-done | bytes 131104 | tf_op jit(solution)/shard_map/ppermute | solution.py:231
  53.9 5.2 %collective-permute-done.17.refs_5_ = f32[64,512]{1,0:T(8,128)S(1)} collective-permute-done((f32[64,512]{1,0:T(8,128)S(1)}, f32[64,512]{1,0:T(8,128)S(1)}, u32[]{:S(2)}, u32[]{:S(2)}) %collective-permute-start.17) | collective-permute-done | bytes 131104 | tf_op jit(solution)/shard_map/ppermute | solution.py:231
  59.4 10.8 %collective-permute-done.15.refs_2_ = f32[64,512]{1,0:T(8,128)S(1)} collective-permute-done((f32[64,512]{1,0:T(8,128)S(1)}, f32[64,512]{1,0:T(8,128)S(1)}, u32[]{:S(2)}, u32[]{:S(2)}) %collective-permute-start.15) | collective-permute-done | bytes 131104 | tf_op jit(solution)/shard_map/ppermute | solution.py:231
  70.2 1.9 %mid.1 = (f32[64,512]{1,0:T(8,128)}, f32[64,512]{1,0:T(8,128)S(1)}, f32[64,768]{1,0:T(8,128)S(1)}) custom-call(s32[1]{0:T(128)} %bitcast.place, f32[64,512]{1,0:T(8,128)S(1)} %add_add_fusion.1.refs_0_, f32[64,512]{1,0:T(8,128)S(1)} %collective-permute-done.14.refs_1_, f32[64,512]{1,0:T(8,128)S(1)} %collective-permute-done.15.refs_2_, ...), custom_call_target="tpu_custom_call" | custom-call | flops 268435456 | bytes 4194304 | tf_op jit(solution)/shard_map/mid/pallas_call | solution.py:176
  72.1 1.8 %collective-permute-start.23 = (f32[64,768]{1,0:T(8,128)S(1)}, f32[64,768]{1,0:T(8,128)S(1)}, u32[]{:S(2)}, u32[]{:S(2)}) collective-permute-start(f32[64,768]{1,0:T(8,128)S(1)} %get-tuple-element.34), channel_id=1, source_target_pairs={{0,16},{4,20},{8,24},{12,28},{16,0},{20,4},{24,8},{28,12},{1,17},{... | collective-permute-start | bytes 589832 | tf_op jit(solution)/shard_map/ppermute | solution.py:226
  73.9 2.2 %collective-permute-start.21 = (f32[64,768]{1,0:T(8,128)S(1)}, f32[64,768]{1,0:T(8,128)S(1)}, u32[]{:S(2)}, u32[]{:S(2)}) collective-permute-start(f32[64,768]{1,0:T(8,128)S(1)} %get-tuple-element.34), channel_id=1, source_target_pairs={{0,24},{4,28},{8,0},{12,4},{16,8},{20,12},{24,16},{28,20},{1,25},{... | collective-permute-start | bytes 589832 | tf_op jit(solution)/shard_map/ppermute | solution.py:226
  76.1 2.0 %collective-permute-start.20 = (f32[64,512]{1,0:T(8,128)S(1)}, f32[64,512]{1,0:T(8,128)S(1)}, u32[]{:S(2)}, u32[]{:S(2)}) collective-permute-start(f32[64,512]{1,0:T(8,128)S(1)} %get-tuple-element.33.refs_0_), channel_id=1, source_target_pairs={{0,4},{4,0},{8,12},{12,8},{16,20},{20,16},{24,28},{28,24},{1,5},{5... | collective-permute-start | bytes 393224 | tf_op jit(solution)/shard_map/ppermute | solution.py:231
  78.0 8.1 %collective-permute-done.20.refs_1_ = f32[64,512]{1,0:T(8,128)S(1)} collective-permute-done((f32[64,512]{1,0:T(8,128)S(1)}, f32[64,512]{1,0:T(8,128)S(1)}, u32[]{:S(2)}, u32[]{:S(2)}) %collective-permute-start.20) | collective-permute-done | bytes 131104 | tf_op jit(solution)/shard_map/ppermute | solution.py:231
  86.1 2.9 %collective-permute-start.24 = (f32[64,512]{1,0:T(8,128)S(1)}, f32[64,512]{1,0:T(8,128)S(1)}, u32[]{:S(2)}, u32[]{:S(2)}) collective-permute-start(f32[64,512]{1,0:T(8,128)S(1)} %collective-permute-done.20.refs_1_), channel_id=1, source_target_pairs={{0,16},{4,20},{8,24},{12,28},{16,0},{20,4},{24,8},{28,12},{1,17},{... | collective-permute-start | bytes 393224 | tf_op jit(solution)/shard_map/ppermute | solution.py:226
  89.6 3.5 %collective-permute-start.28 = (f32[64,256]{1,0:T(8,128)S(1)}, f32[64,256]{1,0:T(8,128)S(1)}, u32[]{:S(2)}, u32[]{:S(2)}) collective-permute-start(f32[64,256]{1,0:T(8,128)S(1)} %slice_add_fusion), channel_id=1, source_target_pairs={{0,4},{4,0},{8,12},{12,8},{16,20},{20,16},{24,28},{28,24},{1,5},{5... | collective-permute-start | bytes 196616 | tf_op jit(solution)/shard_map/ppermute | solution.py:231
  93.6 1.4 %collective-permute-done.22.refs_3_ = f32[64,512]{1,0:T(8,128)S(1)} collective-permute-done((f32[64,512]{1,0:T(8,128)S(1)}, f32[64,512]{1,0:T(8,128)S(1)}, u32[]{:S(2)}, u32[]{:S(2)}) %collective-permute-start.22) | collective-permute-done | bytes 131104 | tf_op jit(solution)/shard_map/ppermute | solution.py:226
  94.9 5.7 %spmm_back.1 = (f32[64,512]{1,0:T(8,128)S(1)}, f32[64,512]{1,0:T(8,128)S(1)}, f32[64,512]{1,0:T(8,128)S(1)}, f32[64,512]{1,0:T(8,128)S(1)}, f32[64,512]{1,0:T(8,...) custom-call(s32[161]{0:T(256)S(1)} %pad_add_fusion.table, ...), custom_call_target="tpu_custom_call" | custom-call | flops 1006632960 | bytes 14680064 | tf_op jit(solution)/shard_map/spmm_back/pallas_call | solution.py:106
  102.8 1.6 %collective-permute-start.35 = (f32[64,768]{1,0:T(8,128)S(1)}, f32[64,768]{1,0:T(8,128)S(1)}, u32[]{:S(2)}, u32[]{:S(2)}) collective-permute-start(f32[64,768]{1,0:T(8,128)S(1)} %shard_map.105), channel_id=1, source_target_pairs={{0,192},{32,224},{64,0},{96,32},{128,64},{160,96},{192,128},{224,1... | collective-permute-start | bytes 589832 | tf_op jit(solution)/shard_map/ppermute | solution.py:226
  105.0 1.4 %collective-permute-start.31 = (f32[64,768]{1,0:T(8,128)S(1)}, f32[64,768]{1,0:T(8,128)S(1)}, u32[]{:S(2)}, u32[]{:S(2)}) collective-permute-start(f32[64,768]{1,0:T(8,128)S(1)} %shard_map.103), channel_id=1, source_target_pairs={{0,128},{32,160},{64,192},{96,224},{128,0},{160,32},{192,64},{224,... | collective-permute-start | bytes 589832 | tf_op jit(solution)/shard_map/ppermute | solution.py:226
  106.5 1.3 %collective-permute-done.27.got = f32[64,512]{1,0:T(8,128)S(1)} collective-permute-done((f32[64,512]{1,0:T(8,128)S(1)}, f32[64,512]{1,0:T(8,128)S(1)}, u32[]{:S(2)}, u32[]{:S(2)}) %collective-permute-start.27) | collective-permute-done | bytes 131104 | tf_op jit(solution)/shard_map/ppermute | solution.py:231
  107.8 2.9 %collective-permute-done.35.refs_2_ = f32[64,768]{1,0:T(8,128)S(1)} collective-permute-done((f32[64,768]{1,0:T(8,128)S(1)}, f32[64,768]{1,0:T(8,128)S(1)}, u32[]{:S(2)}, u32[]{:S(2)}) %collective-permute-start.35) | collective-permute-done | bytes 196640 | tf_op jit(solution)/shard_map/ppermute | solution.py:226
  110.7 6.2 %collective-permute-done.33.refs_1_ = f32[64,768]{1,0:T(8,128)S(1)} collective-permute-done((f32[64,768]{1,0:T(8,128)S(1)}, f32[64,768]{1,0:T(8,128)S(1)}, u32[]{:S(2)}, u32[]{:S(2)}) %collective-permute-start.33) | collective-permute-done | bytes 196640 | tf_op jit(solution)/shard_map/ppermute | solution.py:226
  (63 shorter events, 9.7 us)
Async XLA Ops:
  0.7 6.9 %collective-permute-start.1 = (f32[64,512]{1,0:T(8,128)}, f32[64,512]{1,0:T(8,128)S(1)}, u32[]{:S(2)}, u32[]{:S(2)}) collective-permute-start(f32[64,512]{1,0:T(8,128)} %source.1), channel_id=1, source_target_pairs={{0,192},{32,224},{64,0},{96,32},{128,64},{160,96},{192,128},{224,1... | collective-permute-start | bytes 393224 | tf_op jit(solution)/shard_map/ppermute | solution.py:226
  3.7 11.8 %collective-permute-start = (f32[64,512]{1,0:T(8,128)}, f32[64,512]{1,0:T(8,128)S(1)}, u32[]{:S(2)}, u32[]{:S(2)}) collective-permute-start(f32[64,512]{1,0:T(8,128)} %source.1), channel_id=1, source_target_pairs={{0,32},{32,0},{64,96},{96,64},{128,160},{160,128},{192,224},{224,1... | collective-permute-start | bytes 393224 | tf_op jit(solution)/shard_map/ppermute | solution.py:231
  3.7 10.1 %collective-permute-start.5 = (f32[64,512]{1,0:T(8,128)}, f32[64,512]{1,0:T(8,128)S(1)}, u32[]{:S(2)}, u32[]{:S(2)}) collective-permute-start(f32[64,512]{1,0:T(8,128)} %source.1), channel_id=1, source_target_pairs={{0,64},{32,96},{64,128},{96,160},{128,192},{160,224},{192,0},{224,... | collective-permute-start | bytes 393224 | tf_op jit(solution)/shard_map/ppermute | solution.py:226
  3.8 10.1 %collective-permute-start.3 = (f32[64,512]{1,0:T(8,128)}, f32[64,512]{1,0:T(8,128)S(1)}, u32[]{:S(2)}, u32[]{:S(2)}) collective-permute-start(f32[64,512]{1,0:T(8,128)} %source.1), channel_id=1, source_target_pairs={{0,128},{32,160},{64,192},{96,224},{128,0},{160,32},{192,64},{224,... | collective-permute-start | bytes 393224 | tf_op jit(solution)/shard_map/ppermute | solution.py:226
  7.6 8.0 %collective-permute-start.2 = (f32[64,512]{1,0:T(8,128)S(1)}, f32[64,512]{1,0:T(8,128)S(1)}, u32[]{:S(2)}, u32[]{:S(2)}) collective-permute-start(f32[64,512]{1,0:T(8,128)S(1)} %collective-permute-done.1.refs_2_), channel_id=1, source_target_pairs={{0,32},{32,0},{64,96},{96,64},{128,160},{160,128},{192,224},{224,1... | collective-permute-start | bytes 393224 | tf_op jit(solution)/shard_map/ppermute | solution.py:231
  21.3 8.9 %collective-permute-start.10 = (f32[64,512]{1,0:T(8,128)S(1)}, f32[64,512]{1,0:T(8,128)S(1)}, u32[]{:S(2)}, u32[]{:S(2)}) collective-permute-start(f32[64,512]{1,0:T(8,128)S(1)} %get-tuple-element.29), channel_id=1, source_target_pairs={{0,8},{4,12},{8,16},{12,20},{16,24},{20,28},{24,0},{28,4},{1,9},{5... | collective-permute-start | bytes 393224 | tf_op jit(solution)/shard_map/ppermute | solution.py:226
  23.4 10.1 %collective-permute-start.11 = (f32[64,512]{1,0:T(8,128)S(1)}, f32[64,512]{1,0:T(8,128)S(1)}, u32[]{:S(2)}, u32[]{:S(2)}) collective-permute-start(f32[64,512]{1,0:T(8,128)S(1)} %get-tuple-element.30), channel_id=1, source_target_pairs={{0,16},{4,20},{8,24},{12,28},{16,0},{20,4},{24,8},{28,12},{1,17},{... | collective-permute-start | bytes 393224 | tf_op jit(solution)/shard_map/ppermute | solution.py:226
  25.2 9.2 %collective-permute-start.12 = (f32[64,512]{1,0:T(8,128)S(1)}, f32[64,512]{1,0:T(8,128)S(1)}, u32[]{:S(2)}, u32[]{:S(2)}) collective-permute-start(f32[64,512]{1,0:T(8,128)S(1)} %get-tuple-element.31), channel_id=1, source_target_pairs={{0,24},{4,28},{8,0},{12,4},{16,8},{20,12},{24,16},{28,20},{1,25},{... | collective-permute-start | bytes 393224 | tf_op jit(solution)/shard_map/ppermute | solution.py:226
  26.2 16.0 %collective-permute-start.7 = (f32[64,512]{1,0:T(8,128)S(1)}, f32[64,512]{1,0:T(8,128)S(1)}, u32[]{:S(2)}, u32[]{:S(2)}) collective-permute-start(f32[64,512]{1,0:T(8,128)S(1)} %get-tuple-element.25), channel_id=1, source_target_pairs={{0,8},{4,12},{8,16},{12,20},{16,24},{20,28},{24,0},{28,4},{1,9},{5... | collective-permute-start | bytes 393224 | tf_op jit(solution)/shard_map/ppermute | solution.py:226
  27.2 16.0 %collective-permute-start.8 = (f32[64,512]{1,0:T(8,128)S(1)}, f32[64,512]{1,0:T(8,128)S(1)}, u32[]{:S(2)}, u32[]{:S(2)}) collective-permute-start(f32[64,512]{1,0:T(8,128)S(1)} %get-tuple-element.26), channel_id=1, source_target_pairs={{0,16},{4,20},{8,24},{12,28},{16,0},{20,4},{24,8},{28,12},{1,17},{... | collective-permute-start | bytes 393224 | tf_op jit(solution)/shard_map/ppermute | solution.py:226
  30.1 15.0 %collective-permute-start.9 = (f32[64,512]{1,0:T(8,128)S(1)}, f32[64,512]{1,0:T(8,128)S(1)}, u32[]{:S(2)}, u32[]{:S(2)}) collective-permute-start(f32[64,512]{1,0:T(8,128)S(1)} %get-tuple-element.27), channel_id=1, source_target_pairs={{0,24},{4,28},{8,0},{12,4},{16,8},{20,12},{24,16},{28,20},{1,25},{... | collective-permute-start | bytes 393224 | tf_op jit(solution)/shard_map/ppermute | solution.py:226
  34.4 12.1 %collective-permute-start.13 = (f32[64,512]{1,0:T(8,128)S(1)}, f32[64,512]{1,0:T(8,128)S(1)}, u32[]{:S(2)}, u32[]{:S(2)}) collective-permute-start(f32[64,512]{1,0:T(8,128)S(1)} %add_add_fusion), channel_id=1, source_target_pairs={{0,4},{4,0},{8,12},{12,8},{16,20},{20,16},{24,28},{28,24},{1,5},{5... | collective-permute-start | bytes 393224 | tf_op jit(solution)/shard_map/ppermute | solution.py:231
  40.7 13.1 %collective-permute-start.18 = (f32[64,512]{1,0:T(8,128)S(1)}, f32[64,512]{1,0:T(8,128)S(1)}, u32[]{:S(2)}, u32[]{:S(2)}) collective-permute-start(f32[64,512]{1,0:T(8,128)S(1)} %copy-done.1), channel_id=1, source_target_pairs={{0,2},{1,3},{2,0},{3,1},{4,6},{5,7},{6,4},{7,5},{8,10},{9,11},{10,... | collective-permute-start | bytes 393224 | tf_op jit(solution)/shard_map/ppermute | solution.py:231
  42.2 16.9 %collective-permute-start.17 = (f32[64,512]{1,0:T(8,128)S(1)}, f32[64,512]{1,0:T(8,128)S(1)}, u32[]{:S(2)}, u32[]{:S(2)}) collective-permute-start(f32[64,512]{1,0:T(8,128)S(1)} %copy-done.1), channel_id=1, source_target_pairs={{0,1},{1,0},{2,3},{3,2},{4,5},{5,4},{6,7},{7,6},{8,9},{9,8},{10,11... | collective-permute-start | bytes 393224 | tf_op jit(solution)/shard_map/ppermute | solution.py:231
  43.2 15.9 %collective-permute-start.19 = (f32[64,512]{1,0:T(8,128)S(1)}, f32[64,512]{1,0:T(8,128)S(1)}, u32[]{:S(2)}, u32[]{:S(2)}) collective-permute-start(f32[64,512]{1,0:T(8,128)S(1)} %copy-done.1), channel_id=1, source_target_pairs={{0,3},{1,2},{2,1},{3,0},{4,7},{5,6},{6,5},{7,4},{8,11},{9,10},{10,... | collective-permute-start | bytes 393224 | tf_op jit(solution)/shard_map/ppermute | solution.py:231
  46.6 12.8 %collective-permute-start.16 = (f32[64,512]{1,0:T(8,128)S(1)}, f32[64,512]{1,0:T(8,128)S(1)}, u32[]{:S(2)}, u32[]{:S(2)}) collective-permute-start(f32[64,512]{1,0:T(8,128)S(1)} %add_add_fusion.1.refs_0_), channel_id=1, source_target_pairs={{0,3},{1,2},{2,1},{3,0},{4,7},{5,6},{6,5},{7,4},{8,11},{9,10},{10,... | collective-permute-start | bytes 393224 | tf_op jit(solution)/shard_map/ppermute | solution.py:231
  51.5 18.7 %collective-permute-start.15 = (f32[64,512]{1,0:T(8,128)S(1)}, f32[64,512]{1,0:T(8,128)S(1)}, u32[]{:S(2)}, u32[]{:S(2)}) collective-permute-start(f32[64,512]{1,0:T(8,128)S(1)} %add_add_fusion.1.refs_0_), channel_id=1, source_target_pairs={{0,2},{1,3},{2,0},{3,1},{4,6},{5,7},{6,4},{7,5},{8,10},{9,11},{10,... | collective-permute-start | bytes 393224 | tf_op jit(solution)/shard_map/ppermute | solution.py:231
  53.8 16.4 %collective-permute-start.14 = (f32[64,512]{1,0:T(8,128)S(1)}, f32[64,512]{1,0:T(8,128)S(1)}, u32[]{:S(2)}, u32[]{:S(2)}) collective-permute-start(f32[64,512]{1,0:T(8,128)S(1)} %add_add_fusion.1.refs_0_), channel_id=1, source_target_pairs={{0,1},{1,0},{2,3},{3,2},{4,5},{5,4},{6,7},{7,6},{8,9},{9,8},{10,11... | collective-permute-start | bytes 393224 | tf_op jit(solution)/shard_map/ppermute | solution.py:231
  72.1 16.9 %collective-permute-start.25 = (f32[64,768]{1,0:T(8,128)S(1)}, f32[64,768]{1,0:T(8,128)S(1)}, u32[]{:S(2)}, u32[]{:S(2)}) collective-permute-start(f32[64,768]{1,0:T(8,128)S(1)} %get-tuple-element.34), channel_id=1, source_target_pairs={{0,8},{4,12},{8,16},{12,20},{16,24},{20,28},{24,0},{28,4},{1,9},{5... | collective-permute-start | bytes 589832 | tf_op jit(solution)/shard_map/ppermute | solution.py:226
  72.1 17.5 %collective-permute-start.23 = (f32[64,768]{1,0:T(8,128)S(1)}, f32[64,768]{1,0:T(8,128)S(1)}, u32[]{:S(2)}, u32[]{:S(2)}) collective-permute-start(f32[64,768]{1,0:T(8,128)S(1)} %get-tuple-element.34), channel_id=1, source_target_pairs={{0,16},{4,20},{8,24},{12,28},{16,0},{20,4},{24,8},{28,12},{1,17},{... | collective-permute-start | bytes 589832 | tf_op jit(solution)/shard_map/ppermute | solution.py:226
  73.9 15.7 %collective-permute-start.21 = (f32[64,768]{1,0:T(8,128)S(1)}, f32[64,768]{1,0:T(8,128)S(1)}, u32[]{:S(2)}, u32[]{:S(2)}) collective-permute-start(f32[64,768]{1,0:T(8,128)S(1)} %get-tuple-element.34), channel_id=1, source_target_pairs={{0,24},{4,28},{8,0},{12,4},{16,8},{20,12},{24,16},{28,20},{1,25},{... | collective-permute-start | bytes 589832 | tf_op jit(solution)/shard_map/ppermute | solution.py:226
  76.1 10.0 %collective-permute-start.20 = (f32[64,512]{1,0:T(8,128)S(1)}, f32[64,512]{1,0:T(8,128)S(1)}, u32[]{:S(2)}, u32[]{:S(2)}) collective-permute-start(f32[64,512]{1,0:T(8,128)S(1)} %get-tuple-element.33.refs_0_), channel_id=1, source_target_pairs={{0,4},{4,0},{8,12},{12,8},{16,20},{20,16},{24,28},{28,24},{1,5},{5... | collective-permute-start | bytes 393224 | tf_op jit(solution)/shard_map/ppermute | solution.py:231
  86.1 7.0 %collective-permute-start.26 = (f32[64,512]{1,0:T(8,128)S(1)}, f32[64,512]{1,0:T(8,128)S(1)}, u32[]{:S(2)}, u32[]{:S(2)}) collective-permute-start(f32[64,512]{1,0:T(8,128)S(1)} %collective-permute-done.20.refs_1_), channel_id=1, source_target_pairs={{0,8},{4,12},{8,16},{12,20},{16,24},{20,28},{24,0},{28,4},{1,9},{5... | collective-permute-start | bytes 393224 | tf_op jit(solution)/shard_map/ppermute | solution.py:226
  86.1 7.4 %collective-permute-start.24 = (f32[64,512]{1,0:T(8,128)S(1)}, f32[64,512]{1,0:T(8,128)S(1)}, u32[]{:S(2)}, u32[]{:S(2)}) collective-permute-start(f32[64,512]{1,0:T(8,128)S(1)} %collective-permute-done.20.refs_1_), channel_id=1, source_target_pairs={{0,16},{4,20},{8,24},{12,28},{16,0},{20,4},{24,8},{28,12},{1,17},{... | collective-permute-start | bytes 393224 | tf_op jit(solution)/shard_map/ppermute | solution.py:226
  89.1 5.9 %collective-permute-start.22 = (f32[64,512]{1,0:T(8,128)S(1)}, f32[64,512]{1,0:T(8,128)S(1)}, u32[]{:S(2)}, u32[]{:S(2)}) collective-permute-start(f32[64,512]{1,0:T(8,128)S(1)} %collective-permute-done.20.refs_1_), channel_id=1, source_target_pairs={{0,24},{4,28},{8,0},{12,4},{16,8},{20,12},{24,16},{28,20},{1,25},{... | collective-permute-start | bytes 393224 | tf_op jit(solution)/shard_map/ppermute | solution.py:226
  89.6 11.7 %collective-permute-start.28 = (f32[64,256]{1,0:T(8,128)S(1)}, f32[64,256]{1,0:T(8,128)S(1)}, u32[]{:S(2)}, u32[]{:S(2)}) collective-permute-start(f32[64,256]{1,0:T(8,128)S(1)} %slice_add_fusion), channel_id=1, source_target_pairs={{0,4},{4,0},{8,12},{12,8},{16,20},{20,16},{24,28},{28,24},{1,5},{5... | collective-permute-start | bytes 196616 | tf_op jit(solution)/shard_map/ppermute | solution.py:231
  100.7 2.1 %collective-permute-start.34 = (f32[64,512]{1,0:T(8,128)S(1)}, f32[64,512]{1,0:T(8,128)S(1)}, u32[]{:S(2)}, u32[]{:S(2)}) collective-permute-start(f32[64,512]{1,0:T(8,128)S(1)} %get-tuple-element.42), channel_id=1, source_target_pairs={{0,32},{32,0},{64,96},{96,64},{128,160},{160,128},{192,224},{224,1... | collective-permute-start | bytes 393224 | tf_op jit(solution)/shard_map/ppermute | solution.py:231
  100.8 3.6 %collective-permute-start.32 = (f32[64,512]{1,0:T(8,128)S(1)}, f32[64,512]{1,0:T(8,128)S(1)}, u32[]{:S(2)}, u32[]{:S(2)}) collective-permute-start(f32[64,512]{1,0:T(8,128)S(1)} %get-tuple-element.40), channel_id=1, source_target_pairs={{0,32},{32,0},{64,96},{96,64},{128,160},{160,128},{192,224},{224,1... | collective-permute-start | bytes 393224 | tf_op jit(solution)/shard_map/ppermute | solution.py:231
  101.3 3.8 %collective-permute-start.30 = (f32[64,512]{1,0:T(8,128)S(1)}, f32[64,512]{1,0:T(8,128)S(1)}, u32[]{:S(2)}, u32[]{:S(2)}) collective-permute-start(f32[64,512]{1,0:T(8,128)S(1)} %get-tuple-element.38), channel_id=1, source_target_pairs={{0,32},{32,0},{64,96},{96,64},{128,160},{160,128},{192,224},{224,1... | collective-permute-start | bytes 393224 | tf_op jit(solution)/shard_map/ppermute | solution.py:231
  102.8 7.9 %collective-permute-start.35 = (f32[64,768]{1,0:T(8,128)S(1)}, f32[64,768]{1,0:T(8,128)S(1)}, u32[]{:S(2)}, u32[]{:S(2)}) collective-permute-start(f32[64,768]{1,0:T(8,128)S(1)} %shard_map.105), channel_id=1, source_target_pairs={{0,192},{32,224},{64,0},{96,32},{128,64},{160,96},{192,128},{224,1... | collective-permute-start | bytes 589832 | tf_op jit(solution)/shard_map/ppermute | solution.py:226
  104.4 12.4 %collective-permute-start.33 = (f32[64,768]{1,0:T(8,128)S(1)}, f32[64,768]{1,0:T(8,128)S(1)}, u32[]{:S(2)}, u32[]{:S(2)}) collective-permute-start(f32[64,768]{1,0:T(8,128)S(1)} %shard_map.104), channel_id=1, source_target_pairs={{0,64},{32,96},{64,128},{96,160},{128,192},{160,224},{192,0},{224,... | collective-permute-start | bytes 589832 | tf_op jit(solution)/shard_map/ppermute | solution.py:226
  105.0 11.8 %collective-permute-start.31 = (f32[64,768]{1,0:T(8,128)S(1)}, f32[64,768]{1,0:T(8,128)S(1)}, u32[]{:S(2)}, u32[]{:S(2)}) collective-permute-start(f32[64,768]{1,0:T(8,128)S(1)} %shard_map.103), channel_id=1, source_target_pairs={{0,128},{32,160},{64,192},{96,224},{128,0},{160,32},{192,64},{224,... | collective-permute-start | bytes 589832 | tf_op jit(solution)/shard_map/ppermute | solution.py:226
  (7 other events, 100.2 us)
